TPU v7x, 32 devices: a whole 2x2x4 slice. The times are simulated.
32 devices in a mesh: row: 4 (over z), col: 8 (over y, x, core).
Axes of the slice: x: 2, y: 2, z: 4, core: 2. Of those that a mesh axis runs over, the one named last changes fastest.
Arguments:
- amplitudes: bfloat16 [2048, 8192], P(('col', 'row')), may hold values from -6 to 6
- integrals: bfloat16 [8192, 8192], P('row', 'col'), may hold values from -0.0625 to 0.0625
- integral_tiles: int32 [64, 64], P('row', 'col'), may hold values from 0 to 1, as said below
- amplitude_tiles: int32 [16, 64], P('col'), may hold values 0 or 1
Outputs:
- ladder: float32 [2048, 8192], P('col', 'row')
Inputs may be any that keep to these rules, and one draw needn't show every extreme that they name: `integral_tiles`: tiles of higher ab index are more often nonzero.
All inputs are finite; a program needn't handle non-finite values. No bound on the sum of `amplitude_tiles` on one device may be relied on, other than what follows from the above.
Results may differ from a plain program's by a relative error of at most 0.0003.
Values may be sent and summed in bfloat16 or wider, within the bound.
No kernel may reach another device: no remote copies, remote signals or barrier semaphores. Data moves between devices by JAX's collectives and lax.ppermute only.
A program may use at most 128 MiB of HBM per device.

v0:
```python
import jax
import jax.numpy as jnp
from jax import lax
from jax.sharding import PartitionSpec as P

TILE = 128


def contract(left, right):
    return lax.dot_general(
        left, right, (((1,), (1,)), ((), ())), preferred_element_type=jnp.float32
    )


def on_device(amplitudes, integrals, integral_tiles, amplitude_tiles):
    local_rows = amplitudes.shape[0]
    tile_rows = jnp.repeat(amplitude_tiles, TILE, axis=0)
    tile_rows = lax.dynamic_slice_in_dim(
        tile_rows, lax.axis_index("row") * local_rows, local_rows, 0
    )
    amp_mask = jnp.repeat(tile_rows, TILE, axis=1).astype(jnp.bfloat16)
    masked_amps = amplitudes * amp_mask
    int_mask = jnp.repeat(jnp.repeat(integral_tiles, TILE, axis=0), TILE, axis=1).astype(
        jnp.bfloat16
    )
    masked_ints = integrals * int_mask
    panel = lax.all_gather(masked_amps, "row", axis=0, tiled=True)
    return contract(panel, lax.all_gather(masked_ints, "col", axis=1, tiled=True))


def solution(mesh):
    return jax.shard_map(
        on_device,
        mesh=mesh,
        in_specs=(P(("col", "row"), None), P("row", "col"), P("row", "col"), P("col", None)),
        out_specs=P("col", "row"),
        check_vma=False,
    )
```

profile of v0, /device:TPU:0, one launch (start us, length us, event | category | flops | bytes accessed | tf_op | source)
XLA Modules:
  0.0 279.3 jit_solution(6280737660417096425)
XLA Ops:
  6.5 0.0 copy-start.1
  6.5 0.0 all-gather.3.cloned.1.call-start
  6.5 0.7 broadcast_in_dim.12
  7.3 0.6 broadcast_in_dim.13
  7.9 2.8 %bitcast_multiply_fusion.1 = bf16[64,8192]{1,0:T(8,128)(2,1)} fusion(bf16[64,8192]{1,0:T(8,128)(2,1)} %param.4, bf16[8,8,64,128]{3,2,1,0:T(8,128)(2,1)S(1)} %bitcast.11), kind=kLoop, calls=%fused_computation.1 | loop fusion | flops 524288 | bytes 3145728 | tf_op jit(solution)/shard_map/mul | solution.py:22
  10.7 0.0 all-gather.3.cloned.1.call-update
  10.7 0.0 all-gather.5.cloned.1.call-start
  10.8 0.0 copy-done.1
  10.8 0.1 copy.5
  10.9 0.0 copy-start
  10.9 0.1 broadcast_in_dim.14
  11.0 5.8 %broadcast_in_dim.15 = bf16[2048,8,128]{2,1,0:T(8,128)(2,1)S(1)} broadcast(bf16[2048,8]{1,0:T(8,128)(2,1)S(1)} %bitcast.12), dimensions={0,1} | broadcast | bytes 4227072 | tf_op jit(solution)/shard_map/broadcast_in_dim | solution.py:23
  16.8 0.0 copy-done
  16.8 2.5 bitcast_multiply_fusion
  19.3 0.0 all-gather.5.cloned.1.call-update
  19.3 75.1 %all-gather.3.cloned.1.call-done = bf16[256,8192]{1,0:T(8,128)(2,1)} async-done(((bf16[64,8192]{1,0:T(8,128)(2,1)}), bf16[256,8192]{1,0:T(8,128)(2,1)}) %all-gather.3.cloned.1.call-update) | async-done | bytes 4194320 | tf_op jit(solution)/shard_map/all_gather | solution.py:27
  94.3 161.3 %all-gather.5.cloned.1.call-done = bf16[2048,8192]{1,0:T(8,128)(2,1)} async-done(((bf16[2048,1024]{1,0:T(8,128)(2,1)}), bf16[2048,8192]{1,0:T(8,128)(2,1)}) %all-gather.5.cloned.1.call-update) | async-done | bytes 33554448 | tf_op jit(solution)/shard_map/all_gather | solution.py:28
  255.6 16.9 %fusion = f32[256,2048]{1,0:T(8,128)} fusion(bf16[256,8192]{1,0:T(8,128)(2,1)} %all-gather.3.cloned.1.call-done, bf16[2048,8192]{1,0:T(8,128)(2,1)} %all-gather.5.cloned.1.call-done), kind=kOutput, calls=%fused_computation.3 | convolution fusion | flops 8589934592 | bytes 39845888 | tf_op jit(solution)/shard_map/dot_general | solution.py:10
  (2 shorter events, 0.0 us)
Async XLA Ops:
  6.5 4.2 %copy-start.1 = (s32[16,8]{0,1:T(8,128)S(1)}, s32[16,8]{0,1:T(8,128)}, u32[]{:S(2)}) copy-start(s32[16,8]{0,1:T(8,128)} %param.6) | copy-start | bytes 1540
  6.5 87.8 %all-gather.3.cloned.1.call-start = ((), (), s32[]{:S(2)}) async-start(), calls=%async_computation | async-start | bytes 5242880 | tf_op jit(solution)/shard_map/all_gather | solution.py:27
  10.7 244.9 %all-gather.5.cloned.1.call-start = ((), (), s32[]{:S(2)}) async-start(), calls=%async_computation.1 | async-start | bytes 37748736 | tf_op jit(solution)/shard_map/all_gather | solution.py:28
  10.9 5.9 %copy-start = (bf16[2048,1024]{1,0:T(8,128)(2,1)S(1)}, bf16[2048,1024]{1,0:T(8,128)(2,1)}, u32[]{:S(2)}) copy-start(bf16[2048,1024]{1,0:T(8,128)(2,1)} %param.5) | copy-start | bytes 12582916
Sparse Core Ops, SparseCore 0:
  10.8 83.4 all-gather.2
  96.2 159.3 all-gather.4
where the time goes:
time: 280 us; the launch traced here: 279 us
  waiting for transfers between devices  236 us (84%)
  matrix products  16.9 us (6%)
  between operations  13.5 us (5%)
  local copies, waits for them, and re-layouts  7.25 us (3%)
  other arithmetic  5.35 us (2%)
    all_gather x1, waiting for transfers between devices, on_device(): lax.all_gather(masked_ints, 'col', axis=1, tiled=True)  161 us
    all_gather x1, waiting for transfers between devices, on_device(): panel = lax.all_gather(masked_amps, 'row', axis=0, tiled=True)  75.1 us
    dot_general x1, matrix products, contract(): lax.dot_general(left, right, (((1,), (1,)), ((), ())), preferred_element_...  16.9 us
    broadcast_in_dim x1, local copies, waits for them, and re-layouts, on_device(): jnp.repeat(jnp.repeat(integral_tiles, TILE, axis=0), TILE, axis=1)  5.78 us
  transfers between devices with their start and end apart: 2, of which 2 were waited for; matrix products, arithmetic and copies ran while one was open for 3% of the time, Pallas kernels for 0%

commit v1 on v0

--- a/solution.py
+++ b/solution.py
@@ -24,7 +24,12 @@
         jnp.bfloat16
     )
     masked_ints = integrals * int_mask
-    panel = lax.all_gather(masked_amps, "row", axis=0, tiled=True)
+    ring = [masked_amps]
+    for hop in range(3):
+        ring.append(lax.ppermute(ring[-1], "row", [(dev, (dev + 1) % 4) for dev in range(4)]))
+    panel = jnp.roll(
+        jnp.concatenate(ring[::-1], axis=0), (lax.axis_index("row") + 1) * ring[0].shape[0], axis=0
+    )
     return contract(panel, lax.all_gather(masked_ints, "col", axis=1, tiled=True))
 
 

time: 280 us -> 206 us (0.74)
  waiting for transfers between devices: 236 us -> 148 us
  local copies, waits for them, and re-layouts: 7.25 us -> 17.5 us
  starting transfers between devices: 0.04 us -> 3.08 us
    all_gather x1, waiting for transfers between devices: 161 us -> 71.6 us  [on_device(): lax.all_gather(masked_ints, 'col', axis=1, tiled=True)]
    ppermute x0 -> x3, waiting for transfers between devices: none -> 76.6 us  [on_device(): lax.ppermute(ring[-1], 'row', [(dev, (dev + 1) % 4) for dev in range(4)])]
    all_gather x1 -> x0, waiting for transfers between devices: 75.1 us -> none  [on_device(): panel = lax.all_gather(masked_amps, 'row', axis=0, tiled=True)]
    unnamed x4 -> x11, local copies, waits for them, and re-layouts: 0.01 us -> 9.86 us
    ppermute x0 -> x3, starting transfers between devices: none -> 3.08 us  [on_device(): lax.ppermute(ring[-1], 'row', [(dev, (dev + 1) % 4) for dev in range(4)])]
  transfers between devices with their start and end apart: 2 -> 4, of which waited for: 2 -> 4; matrix products, arithmetic and copies ran while one was open for 3% -> 6% of each run, Pallas kernels for 0% -> 0%
where the time goes in v1:
time: 206 us; the launch traced here: 205 us
  waiting for transfers between devices  148 us (72%)
  local copies, waits for them, and re-layouts  17.5 us (8%)
  matrix products  16.9 us (8%)
  between operations  13.5 us (7%)
  other arithmetic  6.14 us (3%)
  starting transfers between devices  3.08 us (1%)
    ppermute x3, waiting for transfers between devices, on_device(): lax.ppermute(ring[-1], 'row', [(dev, (dev + 1) % 4) for dev in range(4)])  76.6 us
    all_gather x1, waiting for transfers between devices, on_device(): lax.all_gather(masked_ints, 'col', axis=1, tiled=True)  71.6 us
    dot_general x1, matrix products, contract(): lax.dot_general(left, right, (((1,), (1,)), ((), ())), preferred_element_...  16.9 us
    unnamed x11, local copies, waits for them, and re-layouts  9.86 us
    broadcast_in_dim x1, local copies, waits for them, and re-layouts, on_device(): jnp.repeat(jnp.repeat(integral_tiles, TILE, axis=0), TILE, axis=1)  5.78 us
    mul x1, other arithmetic, on_device(): masked_ints = integrals * int_mask  4.75 us
  transfers between devices with their start and end apart: 4, of which 4 were waited for; matrix products, arithmetic and copies ran while one was open for 6% of the time, Pallas kernels for 0%

profile of v1, /device:TPU:0, one launch (start us, length us, event | category | flops | bytes accessed | tf_op | source)
XLA Modules:
  0.0 205.4 jit_solution(3931129885539760497)
XLA Ops:
  6.5 0.0 all-gather.2.cloned.1.call-start
  6.5 0.7 convert_element_type.20
  7.2 0.1 copy.5
  7.3 0.1 broadcast_in_dim.14
  7.4 5.8 %broadcast_in_dim.15 = bf16[2048,8,128]{2,1,0:T(8,128)(2,1)S(1)} broadcast(bf16[2048,8]{1,0:T(8,128)(2,1)S(1)} %bitcast.11), dimensions={0,1} | broadcast | bytes 4227072 | tf_op jit(solution)/shard_map/broadcast_in_dim | solution.py:23
  13.2 0.0 copy-start.1
  13.2 0.0 copy-start
  13.2 4.8 %bitcast_multiply_fusion = bf16[2048,1024]{1,0:T(8,128)(2,1)} fusion(bf16[2048,1024]{1,0:T(8,128)(2,1)} %param.5, bf16[256,8,8,128]{3,2,1,0:T(8,128)(2,1)S(1)} %bitcast.9), kind=kLoop, calls=%fused_computation | loop fusion | flops 2097152 | bytes 12582912 | tf_op jit(solution)/shard_map/mul | solution.py:26
  18.0 0.0 all-gather.2.cloned.1.call-update
  18.0 0.0 copy-done.1
  18.0 0.6 broadcast_in_dim.13
  18.6 0.0 copy-done
  18.7 0.7 bitcast_multiply_fusion.1
  19.4 3.1 %collective-permute-start = (bf16[64,8192]{1,0:T(8,128)(2,1)S(1)}, bf16[64,8192]{1,0:T(8,128)(2,1)S(1)}, u32[]{:S(2)}, u32[]{:S(2)}) collective-permute-start(bf16[64,8192]{1,0:T(8,128)(2,1)S(1)} %bitcast_multiply_fusion.1), channel_id=1, source_target_pairs={{0,8},{8,16},{16,24},{24,0},{1,9},{9,17},{17,25},{25,1},{2,10},{10... | collective-permute-start | bytes 3145736 | tf_op jit(solution)/shard_map/ppermute | solution.py:29
  22.4 25.2 %collective-permute-done = bf16[64,8192]{1,0:T(8,128)(2,1)S(1)} collective-permute-done((bf16[64,8192]{1,0:T(8,128)(2,1)S(1)}, bf16[64,8192]{1,0:T(8,128)(2,1)S(1)}, u32[]{:S(2)}, u32[]{:S(2)}) %collective-permute-start) | collective-permute-done | bytes 1048608 | tf_op jit(solution)/shard_map/ppermute | solution.py:29
  47.6 0.0 collective-permute-start.1
  47.6 26.1 %collective-permute-done.1 = bf16[64,8192]{1,0:T(8,128)(2,1)S(1)} collective-permute-done((bf16[64,8192]{1,0:T(8,128)(2,1)S(1)}, bf16[64,8192]{1,0:T(8,128)(2,1)S(1)}, u32[]{:S(2)}, u32[]{:S(2)}) %collective-permute-start.1) | collective-permute-done | bytes 1048608 | tf_op jit(solution)/shard_map/ppermute | solution.py:29
  73.8 0.0 collective-permute-start.2
  73.8 25.3 %collective-permute-done.2 = bf16[64,8192]{1,0:T(8,128)(2,1)} collective-permute-done((bf16[64,8192]{1,0:T(8,128)(2,1)S(1)}, bf16[64,8192]{1,0:T(8,128)(2,1)}, u32[]{:S(2)}, u32[]{:S(2)}) %collective-permute-start.2) | collective-permute-done | bytes 1048608 | tf_op jit(solution)/shard_map/ppermute | solution.py:29
  99.1 2.3 %constant_dynamic-update-slice_fusion.7 = bf16[512,8192]{1,0:T(8,128)(2,1)} fusion(bf16[64,8192]{1,0:T(8,128)(2,1)} %collective-permute-done.2), kind=kLoop, calls=%fused_computation.12 | loop fusion | bytes 2097152
  101.4 1.1 constant_dynamic-update-slice_fusion.6
  102.4 1.0 constant_dynamic-update-slice_fusion.5
  103.5 1.1 constant_dynamic-update-slice_fusion.4
  104.6 2.3 %constant_dynamic-update-slice_fusion.3 = bf16[512,8192]{1,0:T(8,128)(2,1)} fusion(bf16[512,8192]{1,0:T(8,128)(2,1)} %constant_dynamic-update-slice_fusion.4, bf16[64,8192]{1,0:T(8,128)(2,1)} %collective-permute-done.2), kind=kLoop, calls=%fused_computation.8 | loop fusion | bytes 2097152
  106.8 1.0 constant_dynamic-update-slice_fusion.2
  107.9 1.1 constant_dynamic-update-slice_fusion.1
  108.9 1.1 constant_dynamic-update-slice_fusion
  110.0 71.6 %all-gather.2.cloned.1.call-done = bf16[2048,8192]{1,0:T(8,128)(2,1)} async-done(((bf16[2048,1024]{1,0:T(8,128)(2,1)}), bf16[2048,8192]{1,0:T(8,128)(2,1)}) %all-gather.2.cloned.1.call-update) | async-done | bytes 33554448 | tf_op jit(solution)/shard_map/all_gather | solution.py:33
  181.6 16.9 %fusion = f32[256,2048]{1,0:T(8,128)} fusion(bf16[2048,8192]{1,0:T(8,128)(2,1)} %all-gather.2.cloned.1.call-done, bf16[512,8192]{1,0:T(8,128)(2,1)} %constant_dynamic-update-slice_fusion, s32[]{:T(128)S(6)} %select_n.18), kind=kOutput, calls=%fused_computation.1 | convolution fusion | flops 8589934592 | bytes 39845892 | tf_op jit(solution)/shard_map/dot_general | solution.py:10
  (2 shorter events, 0.0 us)
Async XLA Ops:
  6.5 175.1 %all-gather.2.cloned.1.call-start = ((), (), s32[]{:S(2)}) async-start(), calls=%async_computation | async-start | bytes 37748736 | tf_op jit(solution)/shard_map/all_gather | solution.py:33
  13.2 4.8 %copy-start.1 = (s32[2,64]{1,0:T(2,128)S(1)}, s32[2,64]{1,0:T(2,128)}, u32[]{:S(2)}) copy-start(s32[2,64]{1,0:T(2,128)} %param.7) | copy-start | bytes 1540
  13.2 5.5 %copy-start = (bf16[64,8192]{1,0:T(8,128)(2,1)S(1)}, bf16[64,8192]{1,0:T(8,128)(2,1)}, u32[]{:S(2)}) copy-start(bf16[64,8192]{1,0:T(8,128)(2,1)} %param.4) | copy-start | bytes 3145732
  19.4 28.3 %collective-permute-start = (bf16[64,8192]{1,0:T(8,128)(2,1)S(1)}, bf16[64,8192]{1,0:T(8,128)(2,1)S(1)}, u32[]{:S(2)}, u32[]{:S(2)}) collective-permute-start(bf16[64,8192]{1,0:T(8,128)(2,1)S(1)} %bitcast_multiply_fusion.1), channel_id=1, source_target_pairs={{0,8},{8,16},{16,24},{24,0},{1,9},{9,17},{17,25},{25,1},{2,10},{10... | collective-permute-start | bytes 3145736 | tf_op jit(solution)/shard_map/ppermute | solution.py:29
  47.6 26.1 %collective-permute-start.1 = (bf16[64,8192]{1,0:T(8,128)(2,1)S(1)}, bf16[64,8192]{1,0:T(8,128)(2,1)S(1)}, u32[]{:S(2)}, u32[]{:S(2)}) collective-permute-start(bf16[64,8192]{1,0:T(8,128)(2,1)S(1)} %collective-permute-done), channel_id=1, source_target_pairs={{0,8},{8,16},{16,24},{24,0},{1,9},{9,17},{17,25},{25,1},{2,10},{10... | collective-permute-start | bytes 3145736 | tf_op jit(solution)/shard_map/ppermute | solution.py:29
  73.8 25.3 %collective-permute-start.2 = (bf16[64,8192]{1,0:T(8,128)(2,1)S(1)}, bf16[64,8192]{1,0:T(8,128)(2,1)}, u32[]{:S(2)}, u32[]{:S(2)}) collective-permute-start(bf16[64,8192]{1,0:T(8,128)(2,1)S(1)} %collective-permute-done.1), channel_id=1, source_target_pairs={{0,8},{8,16},{16,24},{24,0},{1,9},{9,17},{17,25},{25,1},{2,10},{10... | collective-permute-start | bytes 3145736 | tf_op jit(solution)/shard_map/ppermute | solution.py:29
Sparse Core Ops, SparseCore 0:
  18.1 163.4 all-gather.1
